TPU v7x, 32 devices: a whole 2x2x4 slice. The times are simulated.
32 devices in a mesh: batch: 8 (over z, y), head: 4 (over x, core).
Axes of the slice: x: 2, y: 2, z: 4, core: 2. Of those that a mesh axis runs over, the one named last changes fastest.
Arguments:
- tokens: bfloat16 [16384, 768], P(('batch', 'head')), may hold values from -6 to 6
- cotangent: bfloat16 [16384, 768], P(('batch', 'head')), may hold values from -6 to 6
- lengths: int32 [32], P('batch'), may hold values from 16 to 512, as said below
- labels: int32 [32], P('batch'), may hold values from 0 to 2
- w_qkv: bfloat16 [768, 2304], replicated, may hold values from -0.21875 to 0.21875
- w_out: bfloat16 [768, 768], replicated, may hold values from -0.875 to 0.875
- w_up: bfloat16 [768, 3072], replicated, may hold values from -0.21875 to 0.21875
- w_down: bfloat16 [3072, 768], replicated, may hold values from -0.109375 to 0.109375
- w_pool: bfloat16 [768, 768], replicated, may hold values from -0.21875 to 0.21875
- w_class: bfloat16 [3, 768], replicated, may hold values from -0.625 to 0.625
- biases: float32 [7, 768], replicated, may hold values from -3 to 3
- norm_gains: float32 [2, 768], replicated, may hold values from 0.25 to 1.75
- bias_up: float32 [3072], replicated, may hold values from -3 to 3
Outputs:
- out: bfloat16 [16384, 768], P(('batch', 'head'))
- grad_tokens: bfloat16 [16384, 768], P(('batch', 'head'))
- losses: float32 [32], P(('batch', 'head'))
- g_qkv: float32 [768, 2304], P(None, ('batch', 'head'))
- g_out: float32 [768, 768], P(None, ('batch', 'head'))
- g_up: float32 [768, 3072], P(None, ('batch', 'head'))
- g_down: float32 [3072, 768], P(None, ('batch', 'head'))
- g_pool: float32 [768, 768], P(None, ('batch', 'head'))
- g_class: float32 [3, 768], P(None, ('batch', 'head'))
- g_biases: float32 [6, 768], P(None, ('batch', 'head'))
- g_gains: float32 [2, 768], P(None, ('batch', 'head'))
- g_bias_up: float32 [3072], P(('batch', 'head'))
- g_pool_bias: float32 [768], P(('batch', 'head'))
Inputs may be any that keep to these rules, and one draw needn't show every extreme that they name: `lengths`: some sequence has exactly 512 and some exactly 16 positions.
All inputs are finite; a program needn't handle non-finite values.
Results may differ from a plain program's by a relative error of at most 0.014.
Values may be sent and summed in bfloat16 or wider, within the bound.
A program may use at most 192 MiB of HBM per device.

v0:
```python
import jax
import jax.numpy as jnp
from jax import lax
from jax.sharding import PartitionSpec as P

D = 768
HEADS = 12
HEAD_DIM = 64
CLASSES = 3
SLOT = 512


def layer_norm(hidden, gain, shift):
    center = hidden - jnp.mean(hidden, axis=-1, keepdims=True)
    spread = jnp.mean(center * center, axis=-1, keepdims=True)
    return center * lax.rsqrt(spread + 1e-12) * gain + shift


def exact_gelu(hidden):
    return jax.nn.gelu(hidden, approximate=False)


def inner(left, right):
    return lax.dot_general(
        left, right, (((0,), (0,)), ((), ())), preferred_element_type=jnp.float32
    )


def against(left, right):
    return lax.dot_general(
        left, right, (((1,), (1,)), ((), ())), preferred_element_type=jnp.float32
    )


def exact(left, right):
    return jnp.dot(left, right, precision=lax.Precision.HIGHEST, preferred_element_type=jnp.float32)


def masked_scores(queries, keys_all, length):
    scores = jnp.einsum(
        "qhd,khd->hqk", queries, keys_all, preferred_element_type=jnp.float32
    ) * HEAD_DIM ** (-0.5)
    allowed = jnp.arange(SLOT) < length
    return jnp.where(allowed[None, None, :], scores, -1e30)


def attend_forward(seq_item):
    packed, length = seq_item
    queries = packed[:, 0]
    keys_all = packed[:, 1]
    values = packed[:, 2]
    scores = masked_scores(queries, keys_all, length)
    row_max = jnp.max(scores, axis=-1, keepdims=True)
    exp_sum = jnp.sum(jnp.exp(scores - row_max), axis=-1, keepdims=True)
    log_total = row_max + jnp.log(exp_sum)
    weights = jnp.exp(scores - log_total).astype(jnp.bfloat16)
    context = jnp.einsum("hqk,khd->qhd", weights, values, preferred_element_type=jnp.float32)
    return (context.astype(jnp.bfloat16), log_total)


def attend_backward(seq_item):
    packed, log_total, d_context, length = seq_item
    queries = packed[:, 0]
    keys_all = packed[:, 1]
    values = packed[:, 2]
    scores = masked_scores(queries, keys_all, length)
    weights = jnp.exp(scores - log_total)
    weights_low = weights.astype(jnp.bfloat16)
    d_weights = jnp.einsum("qhd,khd->hqk", d_context, values, preferred_element_type=jnp.float32)
    d_values = jnp.einsum(
        "hqk,qhd->khd", weights_low, d_context, preferred_element_type=jnp.float32
    )
    row_dot = jnp.sum(weights * d_weights, axis=-1, keepdims=True)
    d_scores = (weights * (d_weights - row_dot)).astype(jnp.bfloat16)
    d_queries = jnp.einsum(
        "hqk,khd->qhd", d_scores, keys_all, preferred_element_type=jnp.float32
    ) * HEAD_DIM ** (-0.5)
    d_keys = jnp.einsum(
        "hqk,qhd->khd", d_scores, queries, preferred_element_type=jnp.float32
    ) * HEAD_DIM ** (-0.5)
    return jnp.stack([d_queries, d_keys, d_values], axis=1).astype(jnp.bfloat16)


def per_device(
    tokens,
    cotangent,
    lengths,
    labels,
    w_qkv,
    w_out,
    w_up,
    w_down,
    w_pool,
    w_class,
    biases,
    norm_gains,
    bias_up,
):
    head_parts = lax.axis_size("head")
    head_rank = lax.axis_index("head")
    tok_rows = tokens.shape[0]
    own_seqs = tok_rows // SLOT
    local_heads = HEADS // head_parts
    slice_width = D // head_parts
    own_lengths = lax.dynamic_slice_in_dim(lengths, head_rank * own_seqs, own_seqs)
    own_labels = lax.dynamic_slice_in_dim(labels, head_rank * own_seqs, own_seqs)
    slot_live = (
        (jnp.arange(SLOT)[None, :] < own_lengths[:, None]).reshape(tok_rows).astype(jnp.float32)
    )
    zeros_key = jnp.zeros((D,), jnp.float32)
    packed = jnp.dot(tokens, w_qkv, preferred_element_type=jnp.float32) + jnp.concatenate(
        [biases[0], zeros_key, biases[1]]
    )
    packed_low = packed.astype(jnp.bfloat16)
    head_view = lax.all_to_all(
        packed_low.reshape(tok_rows, 3, head_parts, slice_width),
        "head",
        split_axis=2,
        concat_axis=0,
        tiled=True,
    )
    seq_view = head_view.reshape(head_parts * own_seqs, SLOT, 3, local_heads, HEAD_DIM)
    context, log_total = lax.map(attend_forward, (seq_view, lengths))
    context_back = lax.all_to_all(
        context.reshape(head_parts * tok_rows, 1, slice_width),
        "head",
        split_axis=0,
        concat_axis=1,
        tiled=True,
    )
    context_tok = context_back.reshape(tok_rows, D)
    attn = jnp.dot(context_tok, w_out, preferred_element_type=jnp.float32) + biases[2]
    first_sum = tokens.astype(jnp.float32) + attn
    norm_one, first_pull = jax.vjp(layer_norm, first_sum, norm_gains[0], biases[3])
    norm_low = norm_one.astype(jnp.bfloat16)
    hidden_up = jnp.dot(norm_low, w_up, preferred_element_type=jnp.float32) + bias_up
    activated_full, gelu_pull = jax.vjp(exact_gelu, hidden_up)
    activated = activated_full.astype(jnp.bfloat16)
    branch = jnp.dot(activated, w_down, preferred_element_type=jnp.float32) + biases[4]
    out_full, second_pull = jax.vjp(layer_norm, norm_one + branch, norm_gains[1], biases[5])
    leading = out_full.reshape(own_seqs, SLOT, D)[:, 0].astype(jnp.bfloat16)
    pooled = jnp.tanh(jnp.dot(leading, w_pool, preferred_element_type=jnp.float32) + biases[6])
    pooled_low = pooled.astype(jnp.bfloat16)
    logits = against(pooled_low, w_class)
    onehot = (jnp.arange(CLASSES)[None, :] == own_labels[:, None]).astype(jnp.float32)
    losses = jax.nn.logsumexp(logits, axis=-1) - jnp.sum(onehot * logits, axis=-1)
    d_logits = jax.nn.softmax(logits, axis=-1) - onehot
    g_class = exact(d_logits.T, pooled_low.astype(jnp.float32))
    d_pre = exact(d_logits, w_class.astype(jnp.float32)) * (1.0 - pooled * pooled)
    g_pool = exact(leading.astype(jnp.float32).T, d_pre)
    g_pool_bias = jnp.sum(d_pre, axis=0)
    d_leading = exact(d_pre, w_pool.astype(jnp.float32).T)
    d_out = cotangent.astype(jnp.float32) * slot_live[:, None]
    d_out = d_out.reshape(own_seqs, SLOT, D).at[:, 0].add(d_leading).reshape(tok_rows, D)
    d_h2, g_gain_two, g_shift_two = second_pull(d_out)
    d_branch = d_h2.astype(jnp.bfloat16)
    g_bias_down = jnp.sum(d_branch.astype(jnp.float32), axis=0)
    g_down = inner(activated, d_branch)
    d_activated = against(d_branch, w_down)
    d_up = gelu_pull(d_activated)[0].astype(jnp.bfloat16)
    g_bias_up = jnp.sum(d_up.astype(jnp.float32), axis=0)
    g_up = inner(norm_low, d_up)
    d_norm_one = d_h2 + against(d_up, w_up)
    d_h1, g_gain_one, g_shift_one = first_pull(d_norm_one)
    d_attn = d_h1.astype(jnp.bfloat16)
    g_bias_out = jnp.sum(d_attn.astype(jnp.float32), axis=0)
    g_out = inner(context_tok, d_attn)
    d_context = against(d_attn, w_out).astype(jnp.bfloat16)
    d_context_heads = lax.all_to_all(
        d_context.reshape(tok_rows, head_parts, slice_width),
        "head",
        split_axis=1,
        concat_axis=0,
        tiled=True,
    )
    d_context_seq = d_context_heads.reshape(head_parts * own_seqs, SLOT, local_heads, HEAD_DIM)
    d_seq = lax.map(attend_backward, (seq_view, log_total, d_context_seq, lengths))
    d_back = lax.all_to_all(
        d_seq.reshape(head_parts * tok_rows, 3, 1, slice_width),
        "head",
        split_axis=0,
        concat_axis=2,
        tiled=True,
    )
    d_packed = d_back.reshape(tok_rows, 3 * D)
    g_qkv = inner(tokens, d_packed)
    column_sums = jnp.sum(d_packed.astype(jnp.float32), axis=0)
    grad_tokens = (d_h1 + against(d_packed, w_qkv)).astype(jnp.bfloat16)
    g_biases = jnp.stack(
        [column_sums[:D], column_sums[2 * D :], g_bias_out, g_shift_one, g_bias_down, g_shift_two]
    )
    g_gains = jnp.stack([g_gain_one, g_gain_two])
    g_qkv, g_out, g_up, g_down, g_pool, g_class, g_biases, g_gains, g_bias_up, g_pool_bias = (
        lax.psum_scatter(g_qkv, ("batch", "head"), scatter_dimension=1, tiled=True),
        lax.psum_scatter(g_out, ("batch", "head"), scatter_dimension=1, tiled=True),
        lax.psum_scatter(g_up, ("batch", "head"), scatter_dimension=1, tiled=True),
        lax.psum_scatter(g_down, ("batch", "head"), scatter_dimension=1, tiled=True),
        lax.psum_scatter(g_pool, ("batch", "head"), scatter_dimension=1, tiled=True),
        lax.psum_scatter(g_class, ("batch", "head"), scatter_dimension=1, tiled=True),
        lax.psum_scatter(g_biases, ("batch", "head"), scatter_dimension=1, tiled=True),
        lax.psum_scatter(g_gains, ("batch", "head"), scatter_dimension=1, tiled=True),
        lax.psum_scatter(g_bias_up, ("batch", "head"), scatter_dimension=0, tiled=True),
        lax.psum_scatter(g_pool_bias, ("batch", "head"), scatter_dimension=0, tiled=True),
    )
    return (
        out_full.astype(jnp.bfloat16),
        grad_tokens,
        losses,
        g_qkv,
        g_out,
        g_up,
        g_down,
        g_pool,
        g_class,
        g_biases,
        g_gains,
        g_bias_up,
        g_pool_bias,
    )


def solution(mesh):
    return jax.shard_map(
        per_device,
        mesh=mesh,
        in_specs=(
            P(("batch", "head"), None),
            P(("batch", "head"), None),
            P("batch"),
            P("batch"),
            P(),
            P(),
            P(),
            P(),
            P(),
            P(),
            P(),
            P(),
            P(),
        ),
        out_specs=(
            P(("batch", "head"), None),
            P(("batch", "head"), None),
            P(("batch", "head")),
            P(None, ("batch", "head")),
            P(None, ("batch", "head")),
            P(None, ("batch", "head")),
            P(None, ("batch", "head")),
            P(None, ("batch", "head")),
            P(None, ("batch", "head")),
            P(None, ("batch", "head")),
            P(None, ("batch", "head")),
            P(("batch", "head")),
            P(("batch", "head")),
        ),
        check_vma=False,
    )
```

profile of v0, /device:TPU:0, one launch (start us, length us, event | category | flops | bytes accessed | tf_op | source)
XLA Modules:
  0.0 791.8 jit_solution(17786111128805935081)
XLA Ops:
  7.2 1.6 slice_reduce_fusion.1
  9.3 4.5 fusion.34
  13.8 4.3 copy.63
  18.1 3.2 copy.64
  21.3 4.7 all-to-all-start
  26.0 29.1 %all-to-all-done = bf16[512,3,4,192]{0,3,1,2:T(8,128)(2,1)} async-done(((bf16[512,3,4,192]{0,3,1,2:T(8,128)(2,1)}), bf16[512,3,4,192]{0,3,1,2:T(8,128)(2,1)}, u32[]{:S(2)}, u32[]{:S(2)}) %all-to-all-start) | async-done | bytes 2359328 | tf_op jit(solution)/shard_map/all_to_all | solution.py:115
  55.1 24.0 %while.23 = (s32[]{:T(128)}, bf16[4,512,3,64]{1,3,2,0:T(8,128)(2,1)}, f32[4,3,512,1]{2,1,3,0:T(4,128)}, bf16[4,512,3,3,64]{1,4,3,2,0:T(8,128)(2,1)}, s32[4]{0:T(128)S(1)}, /*index=5*/s32[]{:T(128)}) while((s32[]{:T(128)}, bf16[4,512,3,64]{1,3,2,0:T(8,128)(2,1)}, f32[4,3,512,1]{2,1,3,0:T(4,128)}, bf16[4,512,3,3,64]{1,4,3,2,0:T(8,128)(2,1)}, ...), condition=%wide.region_3.4_spmd, body=%wide.region_0.3_spmd.sunk | while | flops 210074624 | bytes 11459673 | solution.py:123
  79.1 2.6 copy.65
  81.8 2.8 reshape.337
  85.1 3.0 reduce.38
  88.1 2.2 copy.87
  90.3 3.9 reshape.384
  94.3 4.2 all-to-all-start.1
  104.6 5.5 all-to-all-done.1
  110.2 4.1 reshape.385
  114.3 5.7 copy.67
  120.1 3.0 all_to_all.48
  124.4 2.7 fusion.56
  128.2 19.6 %multiply_convert_fusion.1 = (bf16[512,3072]{1,0:T(8,128)(2,1)S(1)}, f32[512,3072]{1,0:T(8,128)}, f32[512,3072]{1,0:T(8,128)}) fusion(f32[3072]{0:T(1024)S(1)} %copy-done.37, bf16[768,3072]{1,0:T(8,128)(2,1)} %param.25, f32[512,768]{1,0:T(8,128)S(1)} %get-tuple-element.165, f32[768]{0:T(1024)S(1)} %copy-done.32, f32[768]{0:T(1024)S(1)} %get-tuple-element.176, ...), kind=kOutput, calls=%fused_computation.50 | convolution fusion | flops 2521694208 | bytes 22042624 | tf_op jit(solution)/shard_map/dot_general | solution.py:136
  148.0 2.8 fusion.57
  155.5 2.0 fusion.45
  157.5 1.9 divide_subtract_fusion
  163.2 3.2 multiply_reduce_fusion.1
  167.2 2.1 fusion.53
  169.3 1.7 broadcast_multiply_fusion
  172.7 9.5 %convert_reduce_fusion = (f32[3072]{0:T(1024)}, bf16[512,3072]{1,0:T(8,128)(2,1)S(1)}) fusion(f32[512,3072]{1,0:T(8,128)} %get-tuple-element.156, f32[512,3072]{1,0:T(8,128)} %get-tuple-element.166, f32[3072]{0:T(1024)} %param.31, bf16[512,768]{1,0:T(8,128)(2,1)S(1)} %get-tuple-element.148, bf16[3072,768]{1,0:T(8,128)(2,1)} %param.26), kind=kOutput, calls=%fused_computation.48 | convolution fusion | flops 2442654720 | bytes 21258240 | tf_op jit(solution)/shard_map/dot_general | solution.py:30
  182.2 7.3 multiply_reduce_fusion.2
  192.4 1.7 convolution_convert_fusion
  194.1 2.3 copy.69
  196.5 4.2 all-to-all-start.2
  200.9 3.6 fusion.60
  204.6 7.8 all-to-all-done.2
  212.4 39.9 %while.24 = (s32[]{:T(128)}, bf16[4,512,3,3,64]{1,4,3,2,0:T(8,128)(2,1)}, bf16[4,512,3,3,64]{1,4,3,2,0:T(8,128)(2,1)}, s32[4]{0:T(128)}, f32[4,3,512,1]{2,1,3,0:...) while((s32[]{:T(128)}, bf16[4,512,3,3,64]{1,4,3,2,0:T(8,128)(2,1)}, ...), condition=%wide.region_16.17_spmd, body=%wide.region_14.16_spmd.sunk | while | flops 512654336 | bytes 27953856 | solution.py:177
  252.3 4.9 copy.70
  257.2 5.9 reshape.346
  263.1 7.0 copy.71
  270.0 53.9 %all_to_all.60 = bf16[2048,3,1,192]{3,1,2,0:T(4,128)(2,1)} all-to-all(bf16[2048,3,1,192]{3,1,2,0:T(4,128)(2,1)} %copy.71), channel_id=1, replica_groups=mesh['batch'=8,'head'=4] {'head'}, dimensions={0} | all-to-all | bytes 4718592 | tf_op jit(solution)/shard_map/all_to_all | solution.py:178
  323.9 7.4 copy.80
  331.3 2.2 copy.73
  335.0 5.0 convolution_bitcast_fusion
  340.2 8.8 %fusion.48 = f32[768,3072]{0,1:T(8,128)} fusion(bf16[512,3072]{1,0:T(8,128)(2,1)} %copy-done.43, f32[512,768]{1,0:T(8,128)} %copy-done.6, f32[768]{0:T(1024)} %get-tuple-element.107, f32[768]{0:T(1024)S(1)} %copy-done.27, f32[512]{0:T(512)} %copy-done.28, f32[512]{0:T(512)S(1)} %copy-done.17), kind=kOutput, calls=%fused_computation.138 | convolution fusion | flops 2417885184 | bytes 14166016 | tf_op jit(solution)/shard_map/dot_general | solution.py:24
  349.1 8.4 %fusion.61 = f32[3072,768]{0,1:T(8,128)} fusion(bf16[512,3072]{1,0:T(8,128)(2,1)} %copy-done.42, bf16[512,768]{1,0:T(8,128)(2,1)} %copy-done.13), kind=kOutput, calls=%fused_computation.148 | convolution fusion | flops 2415919104 | bytes 13369344 | tf_op jit(solution)/shard_map/dot_general | solution.py:24
  365.2 2.7 convert_reduce_fusion.1
  375.8 42.2 %all-reduce.5 = (f32[3,768]{1,0:T(4,128)}, f32[6,768]{1,0:T(8,128)}, f32[2,768]{1,0:T(2,128)}, f32[3072]{0:T(1024)}, f32[768]{0:T(1024)}) all-reduce(f32[3,768]{1,0:T(4,128)S(1)} %broadcast_multiply_fusion.1, f32[6,768]{1,0:T(8,128)} %stack.38, ...), channel_id=7, replica_groups=mesh['batch'=8,'head'=4] {'batch','head'}, use_global_device_ids=true, to_apply=%region_24.25.clone | all-reduce | flops 12288 | bytes 98304
  424.6 5.1 add_convert_fusion.1
  429.7 70.9 %reduce-scatter.9.cloned.1.call-done = f32[768,72]{0,1:T(8,128)} async-done(((f32[768,2304]{0,1:T(8,128)}), f32[768,72]{0,1:T(8,128)}) %reduce-scatter.9.cloned.1.call-update) | async-done | bytes 221200 | tf_op jit(solution)/shard_map/reduce_scatter | solution.py:194
  500.6 142.2 %reduce-scatter.13.cloned.1.call-done = f32[768,96]{0,1:T(8,128)} async-done(((f32[768,3072]{0,1:T(8,128)}), f32[768,96]{0,1:T(8,128)}) %reduce-scatter.13.cloned.1.call-update) | async-done | bytes 294928 | tf_op jit(solution)/shard_map/reduce_scatter | solution.py:196
  642.8 140.9 %reduce-scatter.15.cloned.1.call-done = f32[3072,24]{0,1:T(8,128)} async-done(((f32[3072,768]{0,1:T(8,128)}), f32[3072,24]{0,1:T(8,128)}) %reduce-scatter.15.cloned.1.call-update) | async-done | bytes 294928 | tf_op jit(solution)/shard_map/reduce_scatter | solution.py:197
  (238 shorter events, 108.5 us)
Async XLA Ops:
  7.2 2.1 copy-start
  8.8 139.0 %copy-start.26 = (f32[768]{0:T(1024)}, f32[768]{0:T(1024)S(1)}, u32[]{:S(2)}) copy-start(f32[768]{0:T(1024)S(1)} %get-tuple-element.176) | copy-start | bytes 9220
  21.3 33.8 %copy-start.40 = (s32[4]{0:T(128)S(1)}, s32[4]{0:T(128)}, u32[]{:S(2)}) copy-start(s32[4]{0:T(128)} %param.21) | copy-start | bytes 52
  21.3 33.8 %all-to-all-start = ((bf16[512,3,4,192]{0,3,1,2:T(8,128)(2,1)}), bf16[512,3,4,192]{0,3,1,2:T(8,128)(2,1)}, u32[]{:S(2)}, u32[]{:S(2)}) async-start(bf16[512,3,4,192]{0,3,1,2:T(8,128)(2,1)} %copy.64), calls=%async_computation | async-start | bytes 4718592 | tf_op jit(solution)/shard_map/all_to_all | solution.py:115
  85.1 15.2 %copy-start.39 = (s32[4]{0:T(128)S(1)}, s32[4]{0:T(128)}, u32[]{:S(2)}) copy-start(s32[4]{0:T(128)} %param.22) | copy-start | bytes 52
  94.3 15.9 %all-to-all-start.1 = ((bf16[4,2,49152]{2,1,0:T(2,128)(2,1)}), bf16[4,2,49152]{2,1,0:T(2,128)(2,1)}, u32[]{:S(2)}, u32[]{:S(2)}) async-start(bf16[4,2,49152]{2,1,0:T(2,128)(2,1)} %reshape.384), calls=%async_computation.1 | async-start | bytes 1572864 | tf_op jit(solution)/shard_map/all_to_all | solution.py:124
  98.5 331.2 %reduce-scatter.17.cloned.1.call-start = ((), (), s32[]{:S(2)}) async-start(), calls=%async_computation.13 | async-start | bytes 2433024 | tf_op jit(solution)/shard_map/reduce_scatter | solution.py:198
  114.3 10.0 %copy-start.34 = (f32[768]{0:T(1024)S(1)}, f32[768]{0:T(1024)}, u32[]{:S(2)}) copy-start(f32[768]{0:T(1024)} %get-tuple-element.108) | copy-start | bytes 9220
  124.3 3.1 copy-start.11
  124.3 3.9 copy-start.32
  124.3 3.9 copy-start.37
  124.4 23.6 %slice-start = ((s8[4718592]{0:T(1024)(128)(4,1)}), s8[4194304]{0:T(1024)(128)(4,1)S(1)}, s32[]{:S(2)}) async-start(s8[4718592]{0:T(1024)(128)(4,1)} %bitcast.202), calls=%async_computation.14 | async-start | bytes 8388608
  127.1 20.8 %copy-start.6 = (f32[512,768]{1,0:T(8,128)}, f32[512,768]{1,0:T(8,128)S(1)}, u32[]{:S(2)}) copy-start(f32[512,768]{1,0:T(8,128)S(1)} %get-tuple-element.165) | copy-start | bytes 4718596
  127.1 20.8 %copy-start.16 = (f32[512]{0:T(512)}, f32[512]{0:T(512)S(1)}, u32[]{:S(2)}) copy-start(f32[512]{0:T(512)S(1)} %broadcast_multiply_fusion.3) | copy-start | bytes 6148
  128.2 19.7 %copy-start.28 = (f32[512]{0:T(512)}, f32[512]{0:T(512)S(1)}, u32[]{:S(2)}) copy-start(f32[512]{0:T(512)S(1)} %fusion.43) | copy-start | bytes 6148
  128.2 19.7 %copy-start.33 = (f32[768]{0:T(1024)S(1)}, f32[768]{0:T(1024)}, u32[]{:S(2)}) copy-start(f32[768]{0:T(1024)} %get-tuple-element.106) | copy-start | bytes 9220
  128.2 19.7 %slice-start.1 = ((s8[4718592]{0:T(1024)(128)(4,1)}), s8[524288]{0:T(1024)(128)(4,1)S(1)}, s32[]{:S(2)}) async-start(s8[4718592]{0:T(1024)(128)(4,1)} %bitcast.202), calls=%async_computation.15 | async-start | bytes 1048576
  147.9 2.9 copy-start.42
  150.7 10.5 %copy-start.1 = (f32[512,768]{1,0:T(8,128)}, f32[512,768]{1,0:T(8,128)S(1)}, u32[]{:S(2)}) copy-start(f32[512,768]{1,0:T(8,128)S(1)} %get-tuple-element.168) | copy-start | bytes 4718596
  150.8 1.9 copy-start.10
  150.8 2.7 copy-start.38
  150.8 10.5 %copy-start.25 = (f32[768]{0:T(1024)S(1)}, f32[768]{0:T(1024)}, u32[]{:S(2)}) copy-start(f32[768]{0:T(1024)} %slice_reduce_fusion) | copy-start | bytes 9220
  163.2 3.9 copy-start.2
  163.2 3.9 copy-start.4
  166.5 2.8 copy-start.30
  166.5 2.8 copy-start.23
  172.6 9.6 %copy-start.13 = (bf16[512,768]{1,0:T(8,128)(2,1)}, bf16[512,768]{1,0:T(8,128)(2,1)S(1)}, u32[]{:S(2)}) copy-start(bf16[512,768]{1,0:T(8,128)(2,1)S(1)} %get-tuple-element.148) | copy-start | bytes 2359300
  172.6 9.6 %copy-start.7 = (f32[512,768]{1,0:T(8,128)S(1)}, f32[512,768]{1,0:T(8,128)}, u32[]{:S(2)}) copy-start(f32[512,768]{1,0:T(8,128)} %copy-done.6) | copy-start | bytes 4718596
  172.6 9.6 %copy-start.9 = (f32[512,768]{1,0:T(8,128)S(1)}, f32[512,768]{1,0:T(8,128)}, u32[]{:S(2)}) copy-start(f32[512,768]{1,0:T(8,128)} %get-tuple-element.154) | copy-start | bytes 4718596
  172.7 9.6 %copy-start.17 = (f32[512]{0:T(512)S(1)}, f32[512]{0:T(512)}, u32[]{:S(2)}) copy-start(f32[512]{0:T(512)} %copy-done.16) | copy-start | bytes 6148
  172.7 9.5 %copy-start.27 = (f32[768]{0:T(1024)S(1)}, f32[768]{0:T(1024)}, u32[]{:S(2)}) copy-start(f32[768]{0:T(1024)} %copy-done.26) | copy-start | bytes 9220
  172.7 9.5 %copy-start.29 = (f32[512]{0:T(512)S(1)}, f32[512]{0:T(512)}, u32[]{:S(2)}) copy-start(f32[512]{0:T(512)} %copy-done.28) | copy-start | bytes 6148
  182.2 7.3 copy-start.43
  182.2 7.3 copy-start.19
  189.5 2.9 copy-start.36
  196.5 15.9 %all-to-all-start.2 = ((bf16[512,4,192]{0,2,1:T(8,128)(2,1)}), bf16[512,4,192]{0,2,1:T(8,128)(2,1)}, u32[]{:S(2)}, u32[]{:S(2)}) async-start(bf16[512,4,192]{0,2,1:T(8,128)(2,1)} %bitcast.198), calls=%async_computation.2 | async-start | bytes 1572864 | tf_op jit(solution)/shard_map/all_to_all | solution.py:169
  200.7 229.0 %reduce-scatter.11.cloned.1.call-start = ((), (), s32[]{:S(2)}) async-start(), calls=%async_computation.10 | async-start | bytes 2433024 | tf_op jit(solution)/shard_map/reduce_scatter | solution.py:195
  204.6 296.0 %reduce-scatter.9.cloned.1.call-start = ((), (), s32[]{:S(2)}) async-start(), calls=%async_computation.9 | async-start | bytes 7299072 | tf_op jit(solution)/shard_map/reduce_scatter | solution.py:194
  212.4 3.4 copy-start.41
  222.4 3.4 copy-start.41
  232.3 3.4 copy-start.41
  242.4 3.4 copy-start.41
  331.3 3.6 copy-start.14
  339.9 302.9 %reduce-scatter.13.cloned.1.call-start = ((), (), s32[]{:S(2)}) async-start(), calls=%async_computation.11 | async-start | bytes 9732096 | tf_op jit(solution)/shard_map/reduce_scatter | solution.py:196
  349.1 434.6 %reduce-scatter.15.cloned.1.call-start = ((), (), s32[]{:S(2)}) async-start(), calls=%async_computation.12 | async-start | bytes 9732096 | tf_op jit(solution)/shard_map/reduce_scatter | solution.py:197
  357.5 2.5 copy-start.22
  357.5 3.8 copy-start.21
  358.2 17.6 %copy-start.24 = (f32[768]{0:T(1024)S(1)}, f32[768]{0:T(1024)}, u32[]{:S(2)}) copy-start(f32[768]{0:T(1024)} %get-tuple-element.172) | copy-start | bytes 9220
  (9 other events, 11.0 us)
Sparse Core Ops, SparseCore 0:
  171.1 100.1 reduce-scatter.16
  278.1 98.0 reduce-scatter.10
  382.4 118.0 reduce-scatter.8
  507.9 134.8 reduce-scatter.12
  649.1 134.5 reduce-scatter.14
where the time goes:
time: 800 us; the launch traced here: 792 us
  waiting for transfers between devices  397 us (50%)
  matrix products  112 us (14%)
  local copies, waits for them, and re-layouts  111 us (14%)
  blocking collectives  96.1 us (12%)
  other arithmetic  42.7 us (5%)
  between operations  18.5 us (2%)
  starting transfers between devices  14.2 us (2%)
    reduce_scatter x1, waiting for transfers between devices, per_device(): lax.psum_scatter(g_up, ('batch', 'head'), scatter_dimension=1, tiled=True)  142 us
    reduce_scatter x1, waiting for transfers between devices, per_device(): lax.psum_scatter(g_down, ('batch', 'head'), scatter_dimension=1, tiled=True)  141 us
    reduce_scatter x1, waiting for transfers between devices, per_device(): lax.psum_scatter(g_qkv, ('batch', 'head'), scatter_dimension=1, tiled=True)  70.9 us
    all_to_all x1, blocking collectives, per_device(): lax.all_to_all(d_seq.reshape(head_parts * tok_rows, 3, 1, slice_width), '...  53.9 us
    unnamed x1, blocking collectives  42.2 us
    all_to_all x1, waiting for transfers between devices, per_device(): lax.all_to_all(packed_low.reshape(tok_rows, 3, head_parts, slice_width),...  29.1 us
    dot_general x4, matrix products, inner(): lax.dot_general(left, right, (((0,), (0,)), ((), ())), preferred_element_...  25.8 us
    dot_general x5, matrix products, against(): lax.dot_general(left, right, (((1,), (1,)), ((), ())), preferred_element_...  24.3 us
  transfers between devices with their start and end apart: 8, of which 6 were waited for; matrix products, arithmetic and copies ran while one was open for 19% of the time, Pallas kernels for 0%

commit v1 on v0

--- a/solution.py
+++ b/solution.py
@@ -112,13 +112,16 @@
         [biases[0], zeros_key, biases[1]]
     )
     packed_low = packed.astype(jnp.bfloat16)
-    head_view = lax.all_to_all(
-        packed_low.reshape(tok_rows, 3, head_parts, slice_width),
-        "head",
-        split_axis=2,
-        concat_axis=0,
-        tiled=True,
-    )
+    array = packed_low.reshape(tok_rows, 3, head_parts, slice_width)
+    ways, here = (lax.axis_size("head"), lax.axis_index("head"))
+    width = array.shape[2] // ways
+    turned = jnp.roll(array, -here * width, axis=2)
+    got = [lax.slice_in_dim(turned, 0, width, axis=2)]
+    for far in range(1, ways):
+        sent = lax.slice_in_dim(turned, far * width, (far + 1) * width, axis=2)
+        got.append(lax.ppermute(sent, "head", [(d, (d + far) % ways) for d in range(ways)]))
+    line = jnp.concatenate(got[::-1], axis=0)
+    head_view = jnp.roll(line, (here + 1) * got[0].shape[0], axis=0)
     seq_view = head_view.reshape(head_parts * own_seqs, SLOT, 3, local_heads, HEAD_DIM)
     context, log_total = lax.map(attend_forward, (seq_view, lengths))
     context_back = lax.all_to_all(

time: 800 us -> 817 us (1.021)
  local copies, waits for them, and re-layouts: 111 us -> 130 us
    all_to_all x1 -> x0, waiting for transfers between devices: 29.1 us -> none  [per_device(): lax.all_to_all(packed_low.reshape(tok_rows, 3, head_parts, slice_width),...]
    ppermute x0 -> x3, waiting for transfers between devices: none -> 25.6 us  [per_device(): lax.ppermute(sent, 'head', [(d, (d + far) % ways) for d in range(ways)])]
    unnamed x98 -> x109, local copies, waits for them, and re-layouts: 23.3 us -> 31.6 us
  transfers between devices with their start and end apart: 8 -> 10, of which waited for: 6 -> 7; matrix products, arithmetic and copies ran while one was open for 19% -> 19% of each run, Pallas kernels for 0% -> 0%
where the time goes in v1:
time: 817 us; the launch traced here: 806 us
  waiting for transfers between devices  391 us (48%)
  local copies, waits for them, and re-layouts  130 us (16%)
  matrix products  112 us (14%)
  blocking collectives  95.2 us (12%)
  other arithmetic  45.9 us (6%)
  between operations  18.5 us (2%)
  starting transfers between devices  12.5 us (2%)
    reduce_scatter x1, waiting for transfers between devices, per_device(): lax.psum_scatter(g_down, ('batch', 'head'), scatter_dimension=1, tiled=True)  142 us
    reduce_scatter x1, waiting for transfers between devices, per_device(): lax.psum_scatter(g_up, ('batch', 'head'), scatter_dimension=1, tiled=True)  141 us
    reduce_scatter x1, waiting for transfers between devices, per_device(): lax.psum_scatter(g_qkv, ('batch', 'head'), scatter_dimension=1, tiled=True)  69.1 us
    all_to_all x1, blocking collectives, per_device(): lax.all_to_all(d_seq.reshape(head_parts * tok_rows, 3, 1, slice_width), '...  53.9 us
    unnamed x1, blocking collectives  41.4 us
    unnamed x109, local copies, waits for them, and re-layouts  31.6 us
    dot_general x4, matrix products, inner(): lax.dot_general(left, right, (((0,), (0,)), ((), ())), preferred_element_...  25.8 us
    ppermute x3, waiting for transfers between devices, per_device(): lax.ppermute(sent, 'head', [(d, (d + far) % ways) for d in range(ways)])  25.6 us
  transfers between devices with their start and end apart: 10, of which 7 were waited for; matrix products, arithmetic and copies ran while one was open for 19% of the time, Pallas kernels for 0%

profile of v1, /device:TPU:0, one launch (start us, length us, event | category | flops | bytes accessed | tf_op | source)
XLA Modules:
  0.0 806.2 jit_solution(4486795924839683524)
XLA Ops:
  9.3 4.5 fusion.34
  13.9 4.3 copy.63
  18.1 2.5 fusion.35
  23.3 2.4 collective-permute-start
  26.5 13.2 %collective-permute-done = bf16[512,3,1,192]{0,3,2,1:T(8,128)(2,1)} collective-permute-done((bf16[512,3,1,192]{0,3,2,1:T(8,128)(2,1)}, bf16[512,3,1,192]{0,3,2,1:T(8,128)(2,1)}, u32[]{:S(2)}, u32[]{:S(2)}) %collective-permute-start) | collective-permute-done | bytes 589856 | tf_op jit(solution)/shard_map/ppermute | solution.py:122
  40.8 12.4 %collective-permute-done.1 = bf16[512,3,1,192]{0,3,2,1:T(8,128)(2,1)} collective-permute-done((bf16[512,3,1,192]{0,3,2,1:T(8,128)(2,1)}, bf16[512,3,1,192]{0,3,2,1:T(8,128)(2,1)}, u32[]{:S(2)}, u32[]{:S(2)}) %collective-permute-start.1) | collective-permute-done | bytes 589856 | tf_op jit(solution)/shard_map/ppermute | solution.py:122
  60.6 6.2 reshape.335
  66.8 3.6 copy.64
  70.4 24.0 %while.23 = (s32[]{:T(128)}, bf16[4,512,3,64]{1,3,2,0:T(8,128)(2,1)}, f32[4,3,512,1]{2,1,3,0:T(4,128)}, bf16[4,512,3,3,64]{1,4,3,2,0:T(8,128)(2,1)}, s32[4]{0:T(128)S(1)}, /*index=5*/s32[]{:T(128)}) while((s32[]{:T(128)}, bf16[4,512,3,64]{1,3,2,0:T(8,128)(2,1)}, f32[4,3,512,1]{2,1,3,0:T(4,128)}, bf16[4,512,3,3,64]{1,4,3,2,0:T(8,128)(2,1)}, ...), condition=%wide.region_3.4_spmd, body=%wide.region_0.3_spmd.sunk | while | flops 210074624 | bytes 11459673 | solution.py:126
  94.4 2.6 copy.65
  97.0 2.8 reshape.336
  100.3 3.0 reduce.38
  103.3 2.2 copy.88
  105.6 3.9 reshape.383
  109.5 4.2 all-to-all-start
  119.5 5.9 all-to-all-done
  125.4 4.1 reshape.384
  129.6 5.7 copy.67
  135.3 3.0 all_to_all.34
  139.6 2.7 fusion.58
  143.5 19.7 %multiply_convert_fusion.1 = (bf16[512,3072]{1,0:T(8,128)(2,1)S(1)}, f32[512,3072]{1,0:T(8,128)}, f32[512,3072]{1,0:T(8,128)}) fusion(f32[3072]{0:T(1024)S(1)} %copy-done.39, bf16[768,3072]{1,0:T(8,128)(2,1)} %param.25, f32[512,768]{1,0:T(8,128)S(1)} %get-tuple-element.190, f32[768]{0:T(1024)S(1)} %copy-done.34, f32[768]{0:T(1024)S(1)} %get-tuple-element.201, ...), kind=kOutput, calls=%fused_computation.50 | convolution fusion | flops 2521694208 | bytes 22042624 | tf_op jit(solution)/shard_map/dot_general | solution.py:139
  163.2 2.8 fusion.59
  170.8 2.0 fusion.46
  172.8 1.9 divide_subtract_fusion
  178.5 3.2 multiply_reduce_fusion.1
  182.5 2.1 fusion.54
  188.0 9.5 %convert_reduce_fusion = (f32[3072]{0:T(1024)}, bf16[512,3072]{1,0:T(8,128)(2,1)S(1)}) fusion(f32[512,3072]{1,0:T(8,128)} %get-tuple-element.178, f32[512,3072]{1,0:T(8,128)} %get-tuple-element.191, f32[3072]{0:T(1024)} %param.31, bf16[512,768]{1,0:T(8,128)(2,1)S(1)} %get-tuple-element.170, bf16[3072,768]{1,0:T(8,128)(2,1)} %param.26), kind=kOutput, calls=%fused_computation.48 | convolution fusion | flops 2442654720 | bytes 21258240 | tf_op jit(solution)/shard_map/dot_general | solution.py:30
  197.6 7.3 multiply_reduce_fusion.2
  209.5 2.3 copy.69
  211.8 4.2 all-to-all-start.1
  216.5 3.6 fusion.62
  220.1 7.6 all-to-all-done.1
  227.7 39.8 %while.24 = (s32[]{:T(128)}, bf16[4,512,3,3,64]{1,4,3,2,0:T(8,128)(2,1)}, bf16[4,512,3,3,64]{1,4,3,2,0:T(8,128)(2,1)}, s32[4]{0:T(128)}, f32[4,3,512,1]{2,1,3,0:...) while((s32[]{:T(128)}, bf16[4,512,3,3,64]{1,4,3,2,0:T(8,128)(2,1)}, ...), condition=%wide.region_16.17_spmd, body=%wide.region_14.16_spmd.sunk | while | flops 512654336 | bytes 27953856 | solution.py:180
  267.6 4.9 copy.71
  272.5 5.9 reshape.345
  278.3 6.9 copy.72
  285.3 53.9 %all_to_all.45 = bf16[2048,3,1,192]{3,1,2,0:T(4,128)(2,1)} all-to-all(bf16[2048,3,1,192]{3,1,2,0:T(4,128)(2,1)} %copy.72), channel_id=1, replica_groups=mesh['batch'=8,'head'=4] {'head'}, dimensions={0} | all-to-all | bytes 4718592 | tf_op jit(solution)/shard_map/all_to_all | solution.py:181
  339.1 7.6 copy.81
  346.7 2.2 copy.74
  350.3 5.0 convolution_bitcast_fusion
  355.5 8.4 %fusion.63 = f32[3072,768]{0,1:T(8,128)} fusion(bf16[512,3072]{1,0:T(8,128)(2,1)} %copy-done.44, bf16[512,768]{1,0:T(8,128)(2,1)} %copy-done.15), kind=kOutput, calls=%fused_computation.161 | convolution fusion | flops 2415919104 | bytes 13369344 | tf_op jit(solution)/shard_map/dot_general | solution.py:24
  364.0 8.8 %fusion.49 = f32[768,3072]{0,1:T(8,128)} fusion(bf16[512,3072]{1,0:T(8,128)(2,1)} %copy-done.45, f32[512,768]{1,0:T(8,128)} %copy-done.8, f32[768]{0:T(1024)} %get-tuple-element.129, f32[768]{0:T(1024)S(1)} %copy-done.29, f32[512]{0:T(512)} %copy-done.30, f32[512]{0:T(512)S(1)} %copy-done.19), kind=kOutput, calls=%fused_computation.150 | convolution fusion | flops 2417885184 | bytes 14166016 | tf_op jit(solution)/shard_map/dot_general | solution.py:24
  382.5 2.7 convert_reduce_fusion.1
  393.1 41.4 %all-reduce.5 = (f32[3,768]{1,0:T(4,128)}, f32[6,768]{1,0:T(8,128)}, f32[2,768]{1,0:T(2,128)}, f32[3072]{0:T(1024)}, f32[768]{0:T(1024)}) all-reduce(f32[3,768]{1,0:T(4,128)S(1)} %broadcast_multiply_fusion.1, f32[6,768]{1,0:T(8,128)} %stack.38, ...), channel_id=7, replica_groups=mesh['batch'=8,'head'=4] {'batch','head'}, use_global_device_ids=true, to_apply=%region_24.25.clone | all-reduce | flops 12288 | bytes 98304
  441.0 5.1 add_convert_fusion.1
  446.1 69.1 %reduce-scatter.9.cloned.1.call-done = f32[768,72]{0,1:T(8,128)} async-done(((f32[768,2304]{0,1:T(8,128)}), f32[768,72]{0,1:T(8,128)}) %reduce-scatter.9.cloned.1.call-update) | async-done | bytes 221200 | tf_op jit(solution)/shard_map/reduce_scatter | solution.py:197
  515.2 142.3 %reduce-scatter.15.cloned.1.call-done = f32[3072,24]{0,1:T(8,128)} async-done(((f32[3072,768]{0,1:T(8,128)}), f32[3072,24]{0,1:T(8,128)}) %reduce-scatter.15.cloned.1.call-update) | async-done | bytes 294928 | tf_op jit(solution)/shard_map/reduce_scatter | solution.py:200
  657.5 140.8 %reduce-scatter.13.cloned.1.call-done = f32[768,96]{0,1:T(8,128)} async-done(((f32[768,3072]{0,1:T(8,128)}), f32[768,96]{0,1:T(8,128)}) %reduce-scatter.13.cloned.1.call-update) | async-done | bytes 294928 | tf_op jit(solution)/shard_map/reduce_scatter | solution.py:199
  (258 shorter events, 126.9 us)
Async XLA Ops:
  8.9 154.3 %copy-start.28 = (f32[768]{0:T(1024)}, f32[768]{0:T(1024)S(1)}, u32[]{:S(2)}) copy-start(f32[768]{0:T(1024)S(1)} %get-tuple-element.201) | copy-start | bytes 9220
  23.3 16.4 %collective-permute-start = (bf16[512,3,1,192]{0,3,2,1:T(8,128)(2,1)}, bf16[512,3,1,192]{0,3,2,1:T(8,128)(2,1)}, u32[]{:S(2)}, u32[]{:S(2)}) collective-permute-start(bf16[512,3,1,192]{0,3,2,1:T(8,128)(2,1)} %get-tuple-element.185), channel_id=1, source_target_pairs={{0,3},{1,0},{2,1},{3,2},{4,7},{5,4},{6,5},{7,6},{8,11},{9,8},{10,9... | collective-permute-start | bytes 1769480 | tf_op jit(solution)/shard_map/ppermute | solution.py:122
  25.7 27.5 %collective-permute-start.1 = (bf16[512,3,1,192]{0,3,2,1:T(8,128)(2,1)}, bf16[512,3,1,192]{0,3,2,1:T(8,128)(2,1)}, u32[]{:S(2)}, u32[]{:S(2)}) collective-permute-start(bf16[512,3,1,192]{0,3,2,1:T(8,128)(2,1)} %get-tuple-element.184), channel_id=1, source_target_pairs={{0,2},{1,3},{2,0},{3,1},{4,6},{5,7},{6,4},{7,5},{8,10},{9,11},{10,... | collective-permute-start | bytes 1769480 | tf_op jit(solution)/shard_map/ppermute | solution.py:122
  26.2 28.1 %collective-permute-start.2 = (bf16[512,3,1,192]{0,3,2,1:T(8,128)(2,1)}, bf16[512,3,1,192]{0,3,2,1:T(8,128)(2,1)}, u32[]{:S(2)}, u32[]{:S(2)}) collective-permute-start(bf16[512,3,1,192]{0,3,2,1:T(8,128)(2,1)} %get-tuple-element.183), channel_id=1, source_target_pairs={{0,1},{1,2},{2,3},{3,0},{4,5},{5,6},{6,7},{7,4},{8,9},{9,10},{10,1... | collective-permute-start | bytes 1769480 | tf_op jit(solution)/shard_map/ppermute | solution.py:122
  26.4 29.0 %copy-start.6 = (bf16[512,3,4,192]{0,3,2,1:T(8,128)(2,1)S(1)}, bf16[512,3,4,192]{0,3,2,1:T(8,128)(2,1)}, u32[]{:S(2)}) copy-start(bf16[512,3,4,192]{0,3,2,1:T(8,128)(2,1)} %copy-done.5) | copy-start | bytes 7077892
  66.8 3.6 copy-start.42
  100.3 14.9 %copy-start.41 = (s32[4]{0:T(128)S(1)}, s32[4]{0:T(128)}, u32[]{:S(2)}) copy-start(s32[4]{0:T(128)} %param.22) | copy-start | bytes 52
  109.5 15.9 %all-to-all-start = ((bf16[4,2,49152]{2,1,0:T(2,128)(2,1)}), bf16[4,2,49152]{2,1,0:T(2,128)(2,1)}, u32[]{:S(2)}, u32[]{:S(2)}) async-start(bf16[4,2,49152]{2,1,0:T(2,128)(2,1)} %reshape.383), calls=%async_computation | async-start | bytes 1572864 | tf_op jit(solution)/shard_map/all_to_all | solution.py:127
  113.7 332.4 %reduce-scatter.17.cloned.1.call-start = ((), (), s32[]{:S(2)}) async-start(), calls=%async_computation.12 | async-start | bytes 2433024 | tf_op jit(solution)/shard_map/reduce_scatter | solution.py:201
  129.6 10.0 %copy-start.36 = (f32[768]{0:T(1024)S(1)}, f32[768]{0:T(1024)}, u32[]{:S(2)}) copy-start(f32[768]{0:T(1024)} %get-tuple-element.130) | copy-start | bytes 9220
  139.6 3.1 copy-start.13
  139.6 3.9 copy-start.34
  139.6 3.9 copy-start.39
  139.6 23.6 %slice-start = ((s8[4718592]{0:T(1024)(128)(4,1)}), s8[4194304]{0:T(1024)(128)(4,1)S(1)}, s32[]{:S(2)}) async-start(s8[4718592]{0:T(1024)(128)(4,1)} %bitcast.201), calls=%async_computation.13 | async-start | bytes 8388608
  142.3 20.8 %copy-start.8 = (f32[512,768]{1,0:T(8,128)}, f32[512,768]{1,0:T(8,128)S(1)}, u32[]{:S(2)}) copy-start(f32[512,768]{1,0:T(8,128)S(1)} %get-tuple-element.190) | copy-start | bytes 4718596
  142.3 20.8 %copy-start.18 = (f32[512]{0:T(512)}, f32[512]{0:T(512)S(1)}, u32[]{:S(2)}) copy-start(f32[512]{0:T(512)S(1)} %broadcast_multiply_fusion.3) | copy-start | bytes 6148
  143.4 19.8 %copy-start.30 = (f32[512]{0:T(512)}, f32[512]{0:T(512)S(1)}, u32[]{:S(2)}) copy-start(f32[512]{0:T(512)S(1)} %fusion.44) | copy-start | bytes 6148
  143.4 19.8 %copy-start.35 = (f32[768]{0:T(1024)S(1)}, f32[768]{0:T(1024)}, u32[]{:S(2)}) copy-start(f32[768]{0:T(1024)} %get-tuple-element.128) | copy-start | bytes 9220
  143.4 19.8 %slice-start.1 = ((s8[4718592]{0:T(1024)(128)(4,1)}), s8[524288]{0:T(1024)(128)(4,1)S(1)}, s32[]{:S(2)}) async-start(s8[4718592]{0:T(1024)(128)(4,1)} %bitcast.201), calls=%async_computation.14 | async-start | bytes 1048576
  163.2 2.9 copy-start.44
  166.0 10.5 %copy-start.1 = (f32[512,768]{1,0:T(8,128)}, f32[512,768]{1,0:T(8,128)S(1)}, u32[]{:S(2)}) copy-start(f32[512,768]{1,0:T(8,128)S(1)} %get-tuple-element.193) | copy-start | bytes 4718596
  166.1 2.7 copy-start.40
  166.1 10.5 %copy-start.27 = (f32[768]{0:T(1024)S(1)}, f32[768]{0:T(1024)}, u32[]{:S(2)}) copy-start(f32[768]{0:T(1024)} %slice_reduce_fusion) | copy-start | bytes 9220
  178.5 3.9 copy-start.2
  178.5 3.9 copy-start.4
  181.8 2.8 copy-start.32
  181.8 2.8 copy-start.25
  187.9 9.6 %copy-start.15 = (bf16[512,768]{1,0:T(8,128)(2,1)}, bf16[512,768]{1,0:T(8,128)(2,1)S(1)}, u32[]{:S(2)}) copy-start(bf16[512,768]{1,0:T(8,128)(2,1)S(1)} %get-tuple-element.170) | copy-start | bytes 2359300
  187.9 9.6 %copy-start.9 = (f32[512,768]{1,0:T(8,128)S(1)}, f32[512,768]{1,0:T(8,128)}, u32[]{:S(2)}) copy-start(f32[512,768]{1,0:T(8,128)} %copy-done.8) | copy-start | bytes 4718596
  187.9 9.6 %copy-start.11 = (f32[512,768]{1,0:T(8,128)S(1)}, f32[512,768]{1,0:T(8,128)}, u32[]{:S(2)}) copy-start(f32[512,768]{1,0:T(8,128)} %get-tuple-element.176) | copy-start | bytes 4718596
  187.9 9.6 %copy-start.19 = (f32[512]{0:T(512)S(1)}, f32[512]{0:T(512)}, u32[]{:S(2)}) copy-start(f32[512]{0:T(512)} %copy-done.18) | copy-start | bytes 6148
  188.0 9.6 %copy-start.29 = (f32[768]{0:T(1024)S(1)}, f32[768]{0:T(1024)}, u32[]{:S(2)}) copy-start(f32[768]{0:T(1024)} %copy-done.28) | copy-start | bytes 9220
  188.0 9.6 %copy-start.31 = (f32[512]{0:T(512)S(1)}, f32[512]{0:T(512)}, u32[]{:S(2)}) copy-start(f32[512]{0:T(512)} %copy-done.30) | copy-start | bytes 6148
  197.5 7.3 copy-start.45
  197.6 7.3 copy-start.21
  204.8 2.9 copy-start.38
  211.8 15.9 %all-to-all-start.1 = ((bf16[512,4,192]{0,2,1:T(8,128)(2,1)}), bf16[512,4,192]{0,2,1:T(8,128)(2,1)}, u32[]{:S(2)}, u32[]{:S(2)}) async-start(bf16[512,4,192]{0,2,1:T(8,128)(2,1)} %bitcast.197), calls=%async_computation.1 | async-start | bytes 1572864 | tf_op jit(solution)/shard_map/all_to_all | solution.py:172
  216.0 230.1 %reduce-scatter.11.cloned.1.call-start = ((), (), s32[]{:S(2)}) async-start(), calls=%async_computation.9 | async-start | bytes 2433024 | tf_op jit(solution)/shard_map/reduce_scatter | solution.py:198
  220.1 295.1 %reduce-scatter.9.cloned.1.call-start = ((), (), s32[]{:S(2)}) async-start(), calls=%async_computation.8 | async-start | bytes 7299072 | tf_op jit(solution)/shard_map/reduce_scatter | solution.py:197
  227.7 3.4 copy-start.43
  237.7 3.4 copy-start.43
  247.7 3.4 copy-start.43
  257.6 3.4 copy-start.43
  346.7 3.6 copy-start.16
  355.3 302.2 %reduce-scatter.15.cloned.1.call-start = ((), (), s32[]{:S(2)}) async-start(), calls=%async_computation.11 | async-start | bytes 9732096 | tf_op jit(solution)/shard_map/reduce_scatter | solution.py:200
  363.9 434.4 %reduce-scatter.13.cloned.1.call-start = ((), (), s32[]{:S(2)}) async-start(), calls=%async_computation.10 | async-start | bytes 9732096 | tf_op jit(solution)/shard_map/reduce_scatter | solution.py:199
  372.8 4.3 copy-start.23
  375.3 17.8 %copy-start.26 = (f32[768]{0:T(1024)S(1)}, f32[768]{0:T(1024)}, u32[]{:S(2)}) copy-start(f32[768]{0:T(1024)} %get-tuple-element.197) | copy-start | bytes 9220
  (13 other events, 17.7 us)
Sparse Core Ops, SparseCore 0:
  186.4 99.4 reduce-scatter.16
  292.6 97.9 reduce-scatter.10
  396.9 118.2 reduce-scatter.8
  522.5 134.9 reduce-scatter.14
  663.9 134.4 reduce-scatter.12
